TPU v7x, 128 devices: a whole 4x4x4 slice. The times are simulated.
128 devices in a mesh: ky: 32 (over y, z_lo, x), kz: 4 (over z_hi, core).
Axes of the slice: x: 4, y: 4, z: 4 (z_hi: 2, z_lo: 2; z = z_hi * 2 + z_lo), core: 2. Of those that a mesh axis runs over, the one named last changes fastest.
Arguments:
- fields: bfloat16 [4, 2, 32, 1024, 1024], P(None, None, None, 'ky', 'kz'), may hold values from -6 to 6
- offsets: int32 [32], replicated, may hold values from 0 to 1023, as said below
Outputs:
- velocity_field: bfloat16 [3, 2, 32, 1024, 1024], P(None, None, 'ky', 'kz')
- scalar_spectrum: bfloat16 [2, 32, 1024, 1024], P(None, None, 'ky', 'kz')
Inputs may be any that keep to these rules, and one draw needn't show every extreme that they name: `offsets`: ky roll of each kx plane; both ends are taken in every draw.
All inputs are finite; a program needn't handle non-finite values.
Results may differ from a plain program's by a relative error of at most 0.0059.
Values may be sent and summed in bfloat16 or wider, within the bound.
A program may use at most 128 MiB of HBM per device.

v0:
```python
import functools
import math

import jax
import jax.numpy as jnp
import numpy as np
from jax import lax
from jax.experimental import pallas as pl
from jax.experimental.pallas import tpu as pltpu
from jax.sharding import PartitionSpec as P

N = 1024
LOW = 32
SCALE = 1.0 / math.sqrt(N)
MESH = pl.DeviceIdType.MESH
BF16 = jnp.bfloat16
F32 = jnp.float32


def factors():
    row = np.arange(LOW, dtype=np.int64)[:, None]
    column = np.arange(N, dtype=np.int64)[None, :]
    coarse = 2.0 * np.pi / N * ((LOW * row * column) % N)
    fine = 2.0 * np.pi / N * ((row * column) % N)
    return np.stack([np.cos(coarse), np.sin(coarse), np.cos(fine), np.sin(fine)]).astype(np.float32)


def dot(a, b):
    return jnp.dot(a, b, preferred_element_type=F32)


def kernel(
    ky_count,
    kz_count,
    offsets_ref,
    fields_ref,
    factor_ref,
    velocity_ref,
    scalar_ref,
    gathered,
    rolled,
    half_done,
    across,
    result,
    turned,
    ky_cos,
    ky_sin,
    kz_cos,
    kz_sin,
    gather_send,
    gather_recv,
    own_sem,
    kz_send,
    kz_recv,
    kz_own,
    back_send,
    back_recv,
    back_own,
    out_sem,
):
    ky = lax.axis_index("ky")
    kz = lax.axis_index("kz")
    rows = N // ky_count
    part = N // kz_count

    barrier = pltpu.get_barrier_semaphore()

    @pl.loop(1, ky_count)
    def _(step):
        pl.semaphore_signal(barrier, inc=1, device_id={"ky": lax.rem(ky + step, ky_count)}, device_id_type=MESH)

    @pl.loop(1, kz_count)
    def _(step):
        pl.semaphore_signal(barrier, inc=1, device_id={"kz": lax.rem(kz + step, kz_count)}, device_id_type=MESH)

    pl.semaphore_wait(barrier, ky_count + kz_count - 2)

    my_rows = pl.ds(pl.multiple_of(ky * rows, rows), rows)
    other_rows = pl.ds(0, N - rows)

    def gather(field):
        pltpu.make_async_copy(fields_ref.at[field, :, ky], gathered.at[field, :, my_rows], own_sem.at[field]).start()

        @pl.loop(1, ky_count)
        def _(step):
            peer = lax.rem(ky + step, ky_count)
            pltpu.make_async_remote_copy(
                src_ref=fields_ref.at[field, :, peer],
                dst_ref=gathered.at[field, :, my_rows],
                send_sem=gather_send.at[field],
                recv_sem=gather_recv.at[field],
                device_id={"ky": peer},
                device_id_type=MESH,
            ).start()

    def gather_all(field):
        others = gathered.at[field, :, other_rows]
        return pltpu.make_async_remote_copy(
            src_ref=others,
            dst_ref=others,
            send_sem=gather_send.at[field],
            recv_sem=gather_recv.at[field],
            device_id={"ky": lax.rem(ky + 1, ky_count)},
            device_id_type=MESH,
        )

    def wait_gathered(field):
        pltpu.make_async_copy(fields_ref.at[field, :, ky], gathered.at[field, :, my_rows], own_sem.at[field]).wait()
        gather_all(field).wait_recv()

    for field in (3, 0, 1, 2):
        gather(field)

    offset = offsets_ref[ky]
    low_row = lax.broadcasted_iota(jnp.int32, (LOW, 1), 0)

    def turn(cos_index, sin_index, multiple, scale):
        angle = lax.rem(low_row * multiple * offset, N).astype(F32) * (2.0 * math.pi / N)
        c, s = jnp.cos(angle) * scale, jnp.sin(angle) * scale
        a, b = factor_ref[cos_index], factor_ref[sin_index]
        turned[cos_index] = a * c - b * s
        turned[sin_index] = a * s + b * c

    turn(0, 1, LOW, SCALE)
    turn(2, 3, 1, 1.0)

    def fill(source, cos_table, sin_table, scale):
        @pl.loop(0, N // LOW)
        def _(block):
            a = source[0, pl.ds(block, 1)] * scale
            b = source[1, pl.ds(block, 1)] * scale
            c, s = source[2], source[3]
            here = pl.ds(pl.multiple_of(block * LOW, LOW), LOW)
            cos_table[here] = (a * c - b * s).astype(BF16)
            sin_table[here] = (a * s + b * c).astype(BF16)

    fill(turned, ky_cos, ky_sin, 1.0)
    fill(factor_ref, kz_cos, kz_sin, SCALE)

    wait_gathered(3)

    @pl.loop(0, kz_count)
    def _(block):
        here = pl.ds(pl.multiple_of(block * part, part), part)
        target = block * part + lax.broadcasted_iota(jnp.int32, (part, N), 0)
        source = lax.rem(target + (N - offset), N)
        chosen = (lax.broadcasted_iota(jnp.int32, (part, N), 1) == source).astype(F32).astype(BF16)
        for side in range(2):
            rolled[side, here] = dot(chosen, gathered[3, side]).astype(BF16)

    def send_across(field):
        @pl.loop(1, kz_count)
        def _(step):
            peer = lax.rem(kz + step, kz_count)
            pltpu.make_async_remote_copy(
                src_ref=half_done.at[field, peer],
                dst_ref=across.at[field, :, :, pl.ds(pl.multiple_of(kz * part, part), part)],
                send_sem=kz_send.at[field],
                recv_sem=kz_recv.at[field],
                device_id={"kz": peer},
                device_id_type=MESH,
            ).start()

        own_across(field).start()

    def own_across(field):
        return pltpu.make_async_copy(
            half_done.at[field, kz],
            across.at[field, :, :, pl.ds(pl.multiple_of(kz * part, part), part)],
            kz_own.at[field],
        )

    def all_across(field):
        others = across.at[field, :, :, pl.ds(0, N - part)]
        return pltpu.make_async_remote_copy(
            src_ref=others,
            dst_ref=others,
            send_sem=kz_send.at[field],
            recv_sem=kz_recv.at[field],
            device_id={"kz": lax.rem(kz + 1, kz_count)},
            device_id_type=MESH,
        )

    for field in range(3):
        wait_gathered(field)

        @pl.loop(0, kz_count)
        def _(block):
            here = pl.ds(pl.multiple_of(block * part, part), part)
            c, s = ky_cos[here], ky_sin[here]
            real, imag = gathered[field, 0], gathered[field, 1]
            half_done[field, block, 0] = (dot(c, real) - dot(s, imag)).astype(BF16)
            half_done[field, block, 1] = (dot(s, real) + dot(c, imag)).astype(BF16)

        send_across(field)

    def own_back():
        return pltpu.make_async_copy(rolled.at[:, my_rows], scalar_ref.at[:, ky], back_own)

    @pl.loop(1, ky_count)
    def _(step):
        peer = lax.rem(ky + step, ky_count)
        pltpu.make_async_remote_copy(
            src_ref=rolled.at[:, pl.ds(pl.multiple_of(peer * rows, rows), rows)],
            dst_ref=scalar_ref.at[:, ky],
            send_sem=back_send,
            recv_sem=back_recv,
            device_id={"ky": peer},
            device_id_type=MESH,
        ).start()

    own_back().start()

    for field in range(3):
        own_across(field).wait()
        all_across(field).wait_recv()

        @pl.loop(0, kz_count)
        def _(block):
            here = pl.ds(pl.multiple_of(block * part, part), part)
            c, s = kz_cos[:, here], kz_sin[:, here]
            real, imag = across[field, 0], across[field, 1]
            result[field, 0, :, here] = (dot(real, c) - dot(imag, s)).astype(BF16)
            result[field, 1, :, here] = (dot(real, s) + dot(imag, c)).astype(BF16)

        pltpu.make_async_copy(result.at[field], velocity_ref.at[field, :, 0], out_sem.at[field]).start()

    others_back = scalar_ref.at[:, pl.ds(0, ky_count - 1)]
    back = pltpu.make_async_remote_copy(
        src_ref=others_back,
        dst_ref=others_back,
        send_sem=back_send,
        recv_sem=back_recv,
        device_id={"ky": lax.rem(ky + 1, ky_count)},
        device_id_type=MESH,
    )
    back.wait_recv()
    own_back().wait()
    for field in range(3):
        pltpu.make_async_copy(result.at[field], velocity_ref.at[field, :, 0], out_sem.at[field]).wait()
    for field in range(4):
        gather_all(field).wait_send()
    for field in range(3):
        all_across(field).wait_send()
    back.wait_send()


def shards(fields, offsets):
    ky_count, kz_count = lax.axis_size("ky"), lax.axis_size("kz")
    rows, part = fields.shape[3], fields.shape[4]
    in_vmem = lambda *shape: pltpu.VMEM(shape, BF16)
    dma = lambda *shape: pltpu.SemaphoreType.DMA(shape)
    return pl.pallas_call(
        functools.partial(kernel, ky_count, kz_count),
        out_shape=(
            jax.ShapeDtypeStruct((3, 2, 1, part, N), BF16),
            jax.ShapeDtypeStruct((2, ky_count, rows, part), BF16),
        ),
        in_specs=[
            pl.BlockSpec(memory_space=pltpu.SMEM),
            pl.BlockSpec(memory_space=pl.ANY),
            pl.BlockSpec(memory_space=pltpu.VMEM),
        ],
        out_specs=(pl.BlockSpec(memory_space=pl.ANY), pl.BlockSpec(memory_space=pl.ANY)),
        scratch_shapes=[
            in_vmem(4, 2, N, part),
            in_vmem(2, N, part),
            in_vmem(3, kz_count, 2, part, part),
            in_vmem(3, 2, part, N),
            in_vmem(3, 2, part, N),
            pltpu.VMEM((4, LOW, N), F32),
            in_vmem(N, N),
            in_vmem(N, N),
            in_vmem(N, N),
            in_vmem(N, N),
            dma(4),
            dma(4),
            dma(4),
            dma(3),
            dma(3),
            dma(3),
            pltpu.SemaphoreType.DMA,
            pltpu.SemaphoreType.DMA,
            pltpu.SemaphoreType.DMA,
            dma(3),
        ],
        compiler_params=pltpu.CompilerParams(
            collective_id=0, has_side_effects=True, vmem_limit_bytes=48 * 2**20
        ),
        name="roll_and_transform",
    )(offsets, fields, jnp.asarray(factors()))


def solution(mesh):
    placed = (P(None, None, None, "ky", "kz"), P())
    return jax.shard_map(
        shards,
        mesh=mesh,
        in_specs=placed,
        out_specs=(P(None, None, "ky", "kz", None), P(None, None, "ky", "kz")),
        check_vma=False,
    )
```

profile of v0, /device:TPU:1, one launch (start us, length us, event | category | flops | bytes accessed | tf_op | source)
XLA Modules:
  0.0 110.5 jit_solution(16376837108727734116)
XLA Ops:
  0.6 0.0 copy-start
  0.6 1.0 copy-done
  1.7 0.0 copy-start.1
  1.7 0.7 copy-done.1
  2.3 105.6 %roll_and_transform.1 = (bf16[3,2,1,256,1024]{4,3,2,1,0:T(8,128)(2,1)S(1)}, bf16[2,32,32,256]{3,2,1,0:T(8,128)(2,1)S(1)}) custom-call(s32[32]{0:T(128)S(1)} %copy-done.1, bf16[4,2,32,32,256]{4,3,2,1,0:T(8,128)(2,1)} %fields_ref.1, f32[4,32,1024]{2,1,0:T(8,128)S(1)} %copy-done), custom_call_target="tpu_custom_call" | custom-call | tf_op jit(solution)/shard_map/roll_and_transform/pallas_call | solution.py:253
  107.9 1.7 %copy.7 = bf16[3,2,1,256,1024]{4,3,2,1,0:T(8,128)(2,1)} copy(bf16[3,2,1,256,1024]{4,3,2,1,0:T(8,128)(2,1)S(1)} %get-tuple-element.4) | data formatting | bytes 6291456
  109.6 1.0 copy.8
Async XLA Ops:
  0.6 1.0 copy-start
  1.7 0.7 copy-start.1
where the time goes:
time: 111 us
  Pallas kernels  106 us (95%)
  local copies, waits for them, and re-layouts  4.33 us (4%)
    pallas_call x1, Pallas kernels, shards(): pl.pallas_call(functools.partial(kernel, ky_count, kz_count), out_shape=(...  106 us
    unnamed x6, local copies, waits for them, and re-layouts  4.33 us

commit v1 on v0

v1 whole, which is shorter than its diff:
```python
import functools
import math

import jax
import jax.numpy as jnp
from jax import lax
from jax.experimental import pallas as pl
from jax.experimental.pallas import tpu as pltpu
from jax.sharding import PartitionSpec as P

N = 1024
LOW = 32
SCALE = 1.0 / math.sqrt(N)
MESH = pl.DeviceIdType.MESH
BF16 = jnp.bfloat16
F32 = jnp.float32
SCALAR = 3
PIECES = (1, 1, 4)


def dot(a, b):
    return jnp.dot(a, b, preferred_element_type=F32)


def kernel(
    ky_count,
    kz_count,
    offsets_ref,
    fields_ref,
    velocity_ref,
    scalar_ref,
    gathered,
    relay,
    rolled,
    back_relay,
    half_done,
    across,
    factor,
    turned,
    ky_cos,
    ky_sin,
    kz_cos,
    kz_sin,
    word,
    relay_send,
    relay_recv,
    relay_own,
    gather_send,
    gather_recv,
    own_sem,
    kz_send,
    kz_recv,
    kz_own,
    over_send,
    over_recv,
    back_send,
    back_recv,
    back_own,
):
    ky = lax.axis_index("ky")
    kz = lax.axis_index("kz")
    rows = N // ky_count
    part = N // kz_count
    plane_count = ky_count // 2

    x, low_z, y = lax.rem(ky, 4), lax.rem(ky // 4, 2), ky // 8

    def at(new_y, new_low_z, new_x):
        return lax.rem(new_y, 4) * 8 + new_low_z * 4 + lax.rem(new_x, 4)

    partner = at(y, 1 - low_z, x)
    beside_x = (at(y, low_z, x + 1), at(y, low_z, x + 3))
    beside_y = (at(y + 1, low_z, x), at(y + 3, low_z, x))

    def kz_peers():
        return [lax.rem(kz // 2 + step // 2, 2) * 2 + lax.rem(kz + step, 2) for step in (2, 3, 1)]

    def signal(sem, **device):
        pl.semaphore_signal(sem, inc=1, device_id=device, device_id_type=MESH)

    def remote(src, dst, send_sem, recv_sem, **device):
        return pltpu.make_async_remote_copy(
            src_ref=src, dst_ref=dst, send_sem=send_sem, recv_sem=recv_sem, device_id=device, device_id_type=MESH
        )

    barrier = pltpu.get_barrier_semaphore()
    for peer in (partner, *beside_x, *beside_y):
        signal(barrier, ky=peer)
    for peer in kz_peers():
        signal(barrier, kz=peer)
    pl.semaphore_wait(barrier, 8)

    def send_over(field):
        for group in range(4):
            remote(
                fields_ref.at[field, :, pl.ds(group * 8 + (1 - low_z) * 4, 4)],
                relay.at[field, :, pl.ds(group * 4, 4)],
                relay_send.at[field],
                relay_recv.at[field],
                ky=partner,
            ).start()

    def all_over(field):
        return remote(
            relay.at[field], relay.at[field], relay_send.at[field], relay_recv.at[field], ky=partner
        )

    for field in (SCALAR, 0, 1, 2):
        send_over(field)

    for turn_index, peers in enumerate((beside_x, beside_y, beside_y, (partner,))):
        for peer in peers:
            signal(word.at[turn_index], ky=peer)
        pl.semaphore_wait(word.at[turn_index], len(peers))

    def rows_of(block):
        return pl.ds(pl.multiple_of(block * rows, rows), rows)

    my_rows, partner_rows = rows_of(ky), rows_of(partner)

    def in_plane(step):
        number = lax.rem(mine + step, plane_count)
        return number, at(number // 4, low_z, number)

    mine = y * 4 + x

    def own_copy(field):
        return pltpu.make_async_copy(fields_ref.at[field, :, ky], gathered.at[field, :, my_rows], own_sem.at[field])

    def relay_copy(field):
        return pltpu.make_async_copy(
            relay.at[field, :, mine], gathered.at[field, :, partner_rows], relay_own.at[field]
        )

    def gather(field):
        own_copy(field).start()

        @pl.loop(1, plane_count)
        def _(step):
            _, peer = in_plane(step)
            remote(
                fields_ref.at[field, :, peer],
                gathered.at[field, :, my_rows],
                gather_send.at[field],
                gather_recv.at[field],
                ky=peer,
            ).start()

    def pass_on(field):
        all_over(field).wait_recv()
        relay_copy(field).start()

        @pl.loop(1, plane_count)
        def _(step):
            number, peer = in_plane(step)
            remote(
                relay.at[field, :, number],
                gathered.at[field, :, partner_rows],
                gather_send.at[field],
                gather_recv.at[field],
                ky=peer,
            ).start()

    def gather_all(field):
        others = gathered.at[field, :, pl.ds(0, (ky_count - 2) * rows)]
        return remote(others, others, gather_send.at[field], gather_recv.at[field], ky=partner)

    def wait_gathered(field):
        own_copy(field).wait()
        relay_copy(field).wait()
        gather_all(field).wait_recv()

    gather(SCALAR)
    gather(0)

    offset = offsets_ref[ky]
    some = LOW // 4

    @pl.loop(0, 4)
    def _(group):
        here = pl.ds(pl.multiple_of(group * some, some), some)
        row = group * some + lax.broadcasted_iota(jnp.int32, (some, N), 0)
        column = lax.broadcasted_iota(jnp.int32, (some, N), 1)
        low_row = group * some + lax.broadcasted_iota(jnp.int32, (some, 128), 0)

        def wave(turns):
            angle = lax.rem(turns, N).astype(F32) * (2.0 * math.pi / N)
            return jnp.cos(angle), jnp.sin(angle)

        for index, multiple, scale in ((0, LOW, SCALE), (2, 1, 1.0)):
            a, b = wave(row * multiple * column)
            a, b = a * scale, b * scale
            c, s = wave(low_row * multiple * offset)
            c, s = c[:, :1], s[:, :1]
            factor[index, here] = a
            factor[index + 1, here] = b
            turned[index, here] = a * c - b * s
            turned[index + 1, here] = a * s + b * c

    def fill(source, cos_table, sin_table):
        @pl.loop(0, N // LOW)
        def _(block):
            a = source[0, pl.ds(block, 1)]
            b = source[1, pl.ds(block, 1)]
            c, s = source[2], source[3]
            here = pl.ds(pl.multiple_of(block * LOW, LOW), LOW)
            cos_table[here] = (a * c - b * s).astype(BF16)
            sin_table[here] = (a * s + b * c).astype(BF16)

    fill(turned, ky_cos, ky_sin)

    pass_on(SCALAR)
    gather(1)
    fill(factor, kz_cos, kz_sin)
    pass_on(0)
    gather(2)

    wait_gathered(SCALAR)

    @pl.loop(0, kz_count)
    def _(block):
        here = pl.ds(pl.multiple_of(block * part, part), part)
        target = block * part + lax.broadcasted_iota(jnp.int32, (part, N), 0)
        source = lax.rem(target + (N - offset), N)
        chosen = (lax.broadcasted_iota(jnp.int32, (part, N), 1) == source).astype(F32).astype(BF16)
        for side in range(2):
            rolled[side, here] = dot(chosen, gathered[SCALAR, side]).astype(BF16)

    for group in range(4):
        remote(
            rolled.at[:, pl.ds(pl.multiple_of(group * 256 + (1 - low_z) * 128, 128), 128)],
            back_relay.at[:, pl.ds(group * 128, 128)],
            over_send,
            over_recv,
            ky=partner,
        ).start()

    own_back = pltpu.make_async_copy(rolled.at[:, my_rows], scalar_ref.at[:, ky], back_own.at[0])
    own_back.start()

    @pl.loop(1, plane_count)
    def _(step):
        _, peer = in_plane(step)
        remote(rolled.at[:, rows_of(peer)], scalar_ref.at[:, ky], back_send, back_recv, ky=peer).start()

    my_part = pl.ds(pl.multiple_of(kz * part, part), part)

    def piece_rows(field, piece):
        size = part // PIECES[field]
        return pl.ds(piece * size, size)

    def own_across(field, piece):
        some_rows = piece_rows(field, piece)
        return pltpu.make_async_copy(
            half_done.at[field, kz, :, some_rows], across.at[field, :, some_rows, my_part], kz_own.at[field, piece]
        )

    def all_across(field, piece):
        others = across.at[field, :, piece_rows(field, piece), pl.ds(0, N - part)]
        return remote(others, others, kz_send.at[field, piece], kz_recv.at[field, piece], kz=kz_peers()[0])

    for field in range(3):
        if field:
            pass_on(field)
        wait_gathered(field)

        @pl.loop(0, kz_count)
        def _(block):
            here = pl.ds(pl.multiple_of(block * part, part), part)
            c, s = ky_cos[here], ky_sin[here]
            real, imag = gathered[field, 0], gathered[field, 1]
            half_done[field, block, 0] = (dot(c, real) - dot(s, imag)).astype(BF16)
            half_done[field, block, 1] = (dot(s, real) + dot(c, imag)).astype(BF16)

        for piece in range(PIECES[field]):
            some_rows = piece_rows(field, piece)
            for peer in kz_peers():
                remote(
                    half_done.at[field, peer, :, some_rows],
                    across.at[field, :, some_rows, my_part],
                    kz_send.at[field, piece],
                    kz_recv.at[field, piece],
                    kz=peer,
                ).start()
            own_across(field, piece).start()

    over = remote(back_relay, back_relay, over_send, over_recv, ky=partner)
    over.wait_recv()
    relay_back = pltpu.make_async_copy(back_relay.at[:, rows_of(mine)], scalar_ref.at[:, partner], back_own.at[1])
    relay_back.start()

    @pl.loop(1, plane_count)
    def _(step):
        number, peer = in_plane(step)
        remote(back_relay.at[:, rows_of(number)], scalar_ref.at[:, partner], back_send, back_recv, ky=peer).start()

    for field in range(3):
        for piece in range(PIECES[field]):
            own_across(field, piece).wait()
            all_across(field, piece).wait_recv()
            some_rows = piece_rows(field, piece)
            size = part // PIECES[field]

            @pl.loop(0, kz_count)
            def _(block):
                here = pl.ds(pl.multiple_of(block * part, part), part)
                both = across[field, :, some_rows].reshape(2 * size, N)
                by_cos, by_sin = dot(both, kz_cos[:, here]), dot(both, kz_sin[:, here])
                velocity_ref[field, 0, 0, some_rows, here] = (by_cos[:size] - by_sin[size:]).astype(BF16)
                velocity_ref[field, 1, 0, some_rows, here] = (by_sin[:size] + by_cos[size:]).astype(BF16)

    others_back = scalar_ref.at[:, pl.ds(0, ky_count - 2)]
    back = remote(others_back, others_back, back_send, back_recv, ky=partner)
    back.wait_recv()
    own_back.wait()
    relay_back.wait()
    for field in range(4):
        all_over(field).wait_send()
        gather_all(field).wait_send()
    for field in range(3):
        for piece in range(PIECES[field]):
            all_across(field, piece).wait_send()
    over.wait_send()
    back.wait_send()


def shards(fields, offsets):
    ky_count, kz_count = lax.axis_size("ky"), lax.axis_size("kz")
    rows, part = fields.shape[3], fields.shape[4]
    in_vmem = lambda *shape: pltpu.VMEM(shape, BF16)
    dma = lambda *shape: pltpu.SemaphoreType.DMA(shape)
    most = max(PIECES)
    return pl.pallas_call(
        functools.partial(kernel, ky_count, kz_count),
        out_shape=(
            jax.ShapeDtypeStruct((3, 2, 1, part, N), BF16),
            jax.ShapeDtypeStruct((2, ky_count, rows, part), BF16),
        ),
        in_specs=[pl.BlockSpec(memory_space=pltpu.SMEM), pl.BlockSpec(memory_space=pl.ANY)],
        out_specs=(pl.BlockSpec(memory_space=pltpu.VMEM), pl.BlockSpec(memory_space=pltpu.VMEM)),
        scratch_shapes=[
            in_vmem(4, 2, N, part),
            in_vmem(4, 2, ky_count // 2, rows, part),
            in_vmem(2, N, part),
            in_vmem(2, N // 2, part),
            in_vmem(3, kz_count, 2, part, part),
            in_vmem(3, 2, part, N),
            pltpu.VMEM((4, LOW, N), F32),
            pltpu.VMEM((4, LOW, N), F32),
            in_vmem(N, N),
            in_vmem(N, N),
            in_vmem(N, N),
            in_vmem(N, N),
            pltpu.SemaphoreType.REGULAR((4,)),
            dma(4),
            dma(4),
            dma(4),
            dma(4),
            dma(4),
            dma(4),
            dma(3, most),
            dma(3, most),
            dma(3, most),
            pltpu.SemaphoreType.DMA,
            pltpu.SemaphoreType.DMA,
            pltpu.SemaphoreType.DMA,
            pltpu.SemaphoreType.DMA,
            dma(2),
        ],
        compiler_params=pltpu.CompilerParams(
            collective_id=0, has_side_effects=True, vmem_limit_bytes=48 * 2**20
        ),
        name="roll_and_transform",
    )(offsets, fields)


def solution(mesh):
    placed = (P(None, None, None, "ky", "kz"), P())
    return jax.shard_map(
        shards,
        mesh=mesh,
        in_specs=placed,
        out_specs=(P(None, None, "ky", "kz", None), P(None, None, "ky", "kz")),
        check_vma=False,
    )
```

time: 111 us -> 105 us (0.946)
  Pallas kernels: 106 us -> 101 us
    pallas_call x1, Pallas kernels: 106 us -> 101 us  [shards(): pl.pallas_call(functools.partial(kernel, ky_count, kz_count), out_shape=(...]
    unnamed x6 -> x4, local copies, waits for them, and re-layouts: 4.33 us -> 3.28 us
where the time goes in v1:
time: 105 us
  Pallas kernels  101 us (96%)
  local copies, waits for them, and re-layouts  3.28 us (3%)
    pallas_call x1, Pallas kernels, shards(): pl.pallas_call(functools.partial(kernel, ky_count, kz_count), out_shape=(...  101 us
    unnamed x4, local copies, waits for them, and re-layouts  3.28 us

profile of v1, /device:TPU:1, one launch (start us, length us, event | category | flops | bytes accessed | tf_op | source)
XLA Modules:
  0.0 104.7 jit_solution(15274716615057505464)
XLA Ops:
  0.6 0.0 copy-start
  0.6 0.6 copy-done
  1.3 100.8 %roll_and_transform.1 = (bf16[3,2,1,256,1024]{4,3,2,1,0:T(8,128)(2,1)S(1)}, bf16[2,32,32,256]{3,2,1,0:T(8,128)(2,1)S(1)}) custom-call(s32[32]{0:T(128)S(1)} %copy-done, bf16[4,2,32,32,256]{4,3,2,1,0:T(8,128)(2,1)} %fields_ref.1), custom_call_target="tpu_custom_call" | custom-call | tf_op jit(solution)/shard_map/roll_and_transform/pallas_call | solution.py:333
  102.1 1.7 %copy.6 = bf16[3,2,1,256,1024]{4,3,2,1,0:T(8,128)(2,1)} copy(bf16[3,2,1,256,1024]{4,3,2,1,0:T(8,128)(2,1)S(1)} %get-tuple-element.4) | data formatting | bytes 6291456
  103.8 1.0 copy.7
Async XLA Ops:
  0.6 0.7 copy-start

commit v2 on v1

--- a/solution.py
+++ b/solution.py
@@ -16,10 +16,42 @@
 F32 = jnp.float32
 SCALAR = 3
 PIECES = (1, 1, 4)
+LAST = (2, 3)
+ROUNDS = 7
 
 
 def dot(a, b):
     return jnp.dot(a, b, preferred_element_type=F32)
+
+
+def along_z(half_ref, cos_ref, sin_ref, out_ref, blocks):
+    size = half_ref.shape[1]
+    width = N // blocks
+
+    @pl.loop(0, blocks)
+    def _(block):
+        here = pl.ds(pl.multiple_of(block * width, width), width)
+        both = half_ref[...].reshape(2 * size, N)
+        by_cos, by_sin = dot(both, cos_ref[:, here]), dot(both, sin_ref[:, here])
+        out_ref[0, :, here] = (by_cos[:size] - by_sin[size:]).astype(BF16)
+        out_ref[1, :, here] = (by_sin[:size] + by_cos[size:]).astype(BF16)
+
+
+def finish(blocks, velocity_ref, scalar_ref, last_ref, cos_ref, sin_ref, velocity_out, scalar_out, result, sems):
+    size = last_ref.shape[1]
+    done = pl.ds(0, N // blocks - size)
+    copies = [
+        pltpu.make_async_copy(velocity_ref.at[0:2], velocity_out.at[0:2, :, 0], sems.at[0]),
+        pltpu.make_async_copy(velocity_ref.at[2, :, done], velocity_out.at[2, :, 0, done], sems.at[1]),
+        pltpu.make_async_copy(scalar_ref, scalar_out, sems.at[2]),
+        pltpu.make_async_copy(result, velocity_out.at[2, :, 0, pl.ds(N // blocks - size, size)], sems.at[3]),
+    ]
+    for copy in copies[:3]:
+        copy.start()
+    along_z(last_ref, cos_ref, sin_ref, result, blocks)
+    copies[3].start()
+    for copy in copies:
+        copy.wait()
 
 
 def kernel(
@@ -29,6 +61,9 @@
     fields_ref,
     velocity_ref,
     scalar_ref,
+    last_ref,
+    kz_cos,
+    kz_sin,
     gathered,
     relay,
     rolled,
@@ -39,8 +74,6 @@
     turned,
     ky_cos,
     ky_sin,
-    kz_cos,
-    kz_sin,
     word,
     relay_send,
     relay_recv,
@@ -69,8 +102,17 @@
         return lax.rem(new_y, 4) * 8 + new_low_z * 4 + lax.rem(new_x, 4)
 
     partner = at(y, 1 - low_z, x)
-    beside_x = (at(y, low_z, x + 1), at(y, low_z, x + 3))
-    beside_y = (at(y + 1, low_z, x), at(y + 3, low_z, x))
+
+    def each_beside_x(act):
+        pl.when(x > 0)(lambda: act(at(y, low_z, x + 3)))
+        pl.when(x < 3)(lambda: act(at(y, low_z, x + 1)))
+
+    def each_beside_y(act):
+        pl.when(y > 0)(lambda: act(at(y + 3, low_z, x)))
+        pl.when(y < 3)(lambda: act(at(y + 1, low_z, x)))
+
+    def count_beside(place):
+        return 2 - jnp.where(place == 0, 1, 0) - jnp.where(place == 3, 1, 0)
 
     def kz_peers():
         return [lax.rem(kz // 2 + step // 2, 2) * 2 + lax.rem(kz + step, 2) for step in (2, 3, 1)]
@@ -84,11 +126,12 @@
         )
 
     barrier = pltpu.get_barrier_semaphore()
-    for peer in (partner, *beside_x, *beside_y):
-        signal(barrier, ky=peer)
+    signal(barrier, ky=partner)
+    each_beside_x(lambda peer: signal(barrier, ky=peer))
+    each_beside_y(lambda peer: signal(barrier, ky=peer))
     for peer in kz_peers():
         signal(barrier, kz=peer)
-    pl.semaphore_wait(barrier, 8)
+    pl.semaphore_wait(barrier, 4 + count_beside(x) + count_beside(y))
 
     def send_over(field):
         for group in range(4):
@@ -108,10 +151,14 @@
     for field in (SCALAR, 0, 1, 2):
         send_over(field)
 
-    for turn_index, peers in enumerate((beside_x, beside_y, beside_y, (partner,))):
-        for peer in peers:
-            signal(word.at[turn_index], ky=peer)
-        pl.semaphore_wait(word.at[turn_index], len(peers))
+    for index in range(3):
+        each_beside_x(lambda peer: signal(word.at[index], ky=peer))
+        pl.semaphore_wait(word.at[index], count_beside(x))
+    for index in range(3, 6):
+        each_beside_y(lambda peer: signal(word.at[index], ky=peer))
+        pl.semaphore_wait(word.at[index], count_beside(y))
+    signal(word.at[6], ky=partner)
+    pl.semaphore_wait(word.at[6], 1)
 
     def rows_of(block):
         return pl.ds(pl.multiple_of(block * rows, rows), rows)
@@ -298,17 +345,13 @@
         for piece in range(PIECES[field]):
             own_across(field, piece).wait()
             all_across(field, piece).wait_recv()
-            some_rows = piece_rows(field, piece)
-            size = part // PIECES[field]
-
-            @pl.loop(0, kz_count)
-            def _(block):
-                here = pl.ds(pl.multiple_of(block * part, part), part)
-                both = across[field, :, some_rows].reshape(2 * size, N)
-                by_cos, by_sin = dot(both, kz_cos[:, here]), dot(both, kz_sin[:, here])
-                velocity_ref[field, 0, 0, some_rows, here] = (by_cos[:size] - by_sin[size:]).astype(BF16)
-                velocity_ref[field, 1, 0, some_rows, here] = (by_sin[:size] + by_cos[size:]).astype(BF16)
-
+            if (field, piece) != LAST:
+                some_rows = piece_rows(field, piece)
+                along_z(
+                    across.at[field, :, some_rows], kz_cos, kz_sin, velocity_ref.at[field, :, some_rows], kz_count
+                )
+
+    last_ref[...] = across[LAST[0], :, piece_rows(*LAST)]
     others_back = scalar_ref.at[:, pl.ds(0, ky_count - 2)]
     back = remote(others_back, others_back, back_send, back_recv, ky=partner)
     back.wait_recv()
@@ -330,14 +373,15 @@
     in_vmem = lambda *shape: pltpu.VMEM(shape, BF16)
     dma = lambda *shape: pltpu.SemaphoreType.DMA(shape)
     most = max(PIECES)
-    return pl.pallas_call(
+    vmem, hbm = pl.BlockSpec(memory_space=pltpu.VMEM), pl.BlockSpec(memory_space=pltpu.HBM)
+    shape = lambda *dims: jax.ShapeDtypeStruct(dims, BF16)
+    scalar_shape = shape(2, ky_count, rows, part)
+    piece = part // PIECES[LAST[0]]
+    held = pl.pallas_call(
         functools.partial(kernel, ky_count, kz_count),
-        out_shape=(
-            jax.ShapeDtypeStruct((3, 2, 1, part, N), BF16),
-            jax.ShapeDtypeStruct((2, ky_count, rows, part), BF16),
-        ),
+        out_shape=(shape(3, 2, part, N), scalar_shape, shape(2, piece, N), shape(N, N), shape(N, N)),
         in_specs=[pl.BlockSpec(memory_space=pltpu.SMEM), pl.BlockSpec(memory_space=pl.ANY)],
-        out_specs=(pl.BlockSpec(memory_space=pltpu.VMEM), pl.BlockSpec(memory_space=pltpu.VMEM)),
+        out_specs=(vmem,) * 5,
         scratch_shapes=[
             in_vmem(4, 2, N, part),
             in_vmem(4, 2, ky_count // 2, rows, part),
@@ -349,9 +393,7 @@
             pltpu.VMEM((4, LOW, N), F32),
             in_vmem(N, N),
             in_vmem(N, N),
-            in_vmem(N, N),
-            in_vmem(N, N),
-            pltpu.SemaphoreType.REGULAR((4,)),
+            pltpu.SemaphoreType.REGULAR((ROUNDS,)),
             dma(4),
             dma(4),
             dma(4),
@@ -368,10 +410,19 @@
             dma(2),
         ],
         compiler_params=pltpu.CompilerParams(
-            collective_id=0, has_side_effects=True, vmem_limit_bytes=48 * 2**20
+            collective_id=0, has_side_effects=True, vmem_limit_bytes=44 * 2**20
         ),
         name="roll_and_transform",
     )(offsets, fields)
+    return pl.pallas_call(
+        functools.partial(finish, kz_count),
+        out_shape=(shape(3, 2, 1, part, N), scalar_shape),
+        in_specs=[vmem] * 5,
+        out_specs=(hbm, hbm),
+        scratch_shapes=[in_vmem(2, piece, N), dma(4)],
+        compiler_params=pltpu.CompilerParams(vmem_limit_bytes=8 * 2**20),
+        name="finish",
+    )(*held)
 
 
 def solution(mesh):

time: 105 us -> 102 us (0.971)
  local copies, waits for them, and re-layouts: 3.28 us -> 0.65 us
    pallas_call x1, Pallas kernels: 101 us -> 98.1 us  [shards(): pl.pallas_call(functools.partial(kernel, ky_count, kz_count), out_shape=(...]
    unnamed x4 -> x2, local copies, waits for them, and re-layouts: 3.28 us -> 0.65 us
    pallas_call x0 -> x1, Pallas kernels: none -> 2.1 us  [shards(): pl.pallas_call(functools.partial(finish, kz_count), out_shape=(shape(3, 2...]
where the time goes in v2:
time: 102 us; the launch traced here: 101 us
  Pallas kernels  100 us (98%)
    pallas_call x1, Pallas kernels, shards(): pl.pallas_call(functools.partial(kernel, ky_count, kz_count), out_shape=(...  98.1 us
    pallas_call x1, Pallas kernels, shards(): pl.pallas_call(functools.partial(finish, kz_count), out_shape=(shape(3, 2...  2.1 us

profile of v2, /device:TPU:1, one launch (start us, length us, event | category | flops | bytes accessed | tf_op | source)
XLA Modules:
  0.0 101.5 jit_solution(6706592669350554619)
XLA Ops:
  0.6 0.0 copy-start
  0.6 0.6 copy-done
  1.3 98.1 %roll_and_transform.1 = (bf16[3,2,256,1024]{3,2,1,0:T(8,128)(2,1)S(1)}, bf16[2,32,32,256]{3,2,1,0:T(8,128)(2,1)S(1)}, bf16[2,64,1024]{2,1,0:T(8,128)(2,1)S(1)}, ...) custom-call(s32[32]{0:T(128)S(1)} %copy-done, bf16[4,2,32,32,256]{4,3,2,1,0:T(8,128)(2,1)} %fields_ref.1), custom_call_target="tpu_custom_call" | custom-call | tf_op jit(solution)/shard_map/roll_and_transform/pallas_call | solution.py:380
  99.4 2.1 %finish.1 = (bf16[3,2,1,256,1024]{4,3,2,1,0:T(8,128)(2,1)}, bf16[2,32,32,256]{3,2,1,0:T(8,128)(2,1)}) custom-call(bf16[3,2,256,1024]{3,2,1,0:T(8,128)(2,1)S(1)} %get-tuple-element.7.velocity_ref, bf16[2,32,32,256]{3,2,1,0:T(8,128)(2,1)S(1)} %get-tuple-element.8.scalar_ref, bf16[2,64,1024]{2,1,0:T(8,128)(2,1)S(1)} %get-tuple-element.9.last_ref, ...), custom_call_target="tpu_custom_call" | custom-call | tf_op jit(solution)/shard_map/finish/pallas_call | solution.py:417
Async XLA Ops:
  0.6 0.7 copy-start

commit v3 on v2

--- a/solution.py
+++ b/solution.py
@@ -16,6 +16,7 @@
 F32 = jnp.float32
 SCALAR = 3
 PIECES = (1, 1, 4)
+FIRST = (0, 1, 2)
 LAST = (2, 3)
 ROUNDS = 7
 
@@ -57,13 +58,14 @@
 def kernel(
     ky_count,
     kz_count,
-    offsets_ref,
+    offsets_hbm,
     fields_ref,
     velocity_ref,
     scalar_ref,
     last_ref,
     kz_cos,
     kz_sin,
+    offsets_ref,
     gathered,
     relay,
     rolled,
@@ -75,6 +77,7 @@
     ky_cos,
     ky_sin,
     word,
+    offsets_sem,
     relay_send,
     relay_recv,
     relay_own,
@@ -138,18 +141,19 @@
             remote(
                 fields_ref.at[field, :, pl.ds(group * 8 + (1 - low_z) * 4, 4)],
                 relay.at[field, :, pl.ds(group * 4, 4)],
-                relay_send.at[field],
+                relay_send,
                 relay_recv.at[field],
                 ky=partner,
             ).start()
 
     def all_over(field):
-        return remote(
-            relay.at[field], relay.at[field], relay_send.at[field], relay_recv.at[field], ky=partner
-        )
+        return remote(relay.at[field], relay.at[field], relay_send, relay_recv.at[field], ky=partner)
 
     for field in (SCALAR, 0, 1, 2):
         send_over(field)
+
+    copy_offsets = pltpu.make_async_copy(offsets_hbm, offsets_ref, offsets_sem)
+    copy_offsets.start()
 
     for index in range(3):
         each_beside_x(lambda peer: signal(word.at[index], ky=peer))
@@ -188,7 +192,7 @@
             remote(
                 fields_ref.at[field, :, peer],
                 gathered.at[field, :, my_rows],
-                gather_send.at[field],
+                gather_send,
                 gather_recv.at[field],
                 ky=peer,
             ).start()
@@ -203,14 +207,14 @@
             remote(
                 relay.at[field, :, number],
                 gathered.at[field, :, partner_rows],
-                gather_send.at[field],
+                gather_send,
                 gather_recv.at[field],
                 ky=peer,
             ).start()
 
     def gather_all(field):
         others = gathered.at[field, :, pl.ds(0, (ky_count - 2) * rows)]
-        return remote(others, others, gather_send.at[field], gather_recv.at[field], ky=partner)
+        return remote(others, others, gather_send, gather_recv.at[field], ky=partner)
 
     def wait_gathered(field):
         own_copy(field).wait()
@@ -220,6 +224,7 @@
     gather(SCALAR)
     gather(0)
 
+    copy_offsets.wait()
     offset = offsets_ref[ky]
     some = LOW // 4
 
@@ -299,12 +304,12 @@
     def own_across(field, piece):
         some_rows = piece_rows(field, piece)
         return pltpu.make_async_copy(
-            half_done.at[field, kz, :, some_rows], across.at[field, :, some_rows, my_part], kz_own.at[field, piece]
+            half_done.at[field, kz, :, some_rows], across.at[field, :, some_rows, my_part], kz_own.at[FIRST[field] + piece]
         )
 
     def all_across(field, piece):
         others = across.at[field, :, piece_rows(field, piece), pl.ds(0, N - part)]
-        return remote(others, others, kz_send.at[field, piece], kz_recv.at[field, piece], kz=kz_peers()[0])
+        return remote(others, others, kz_send, kz_recv.at[FIRST[field] + piece], kz=kz_peers()[0])
 
     for field in range(3):
         if field:
@@ -325,8 +330,8 @@
                 remote(
                     half_done.at[field, peer, :, some_rows],
                     across.at[field, :, some_rows, my_part],
-                    kz_send.at[field, piece],
-                    kz_recv.at[field, piece],
+                    kz_send,
+                    kz_recv.at[FIRST[field] + piece],
                     kz=peer,
                 ).start()
             own_across(field, piece).start()
@@ -357,12 +362,11 @@
     back.wait_recv()
     own_back.wait()
     relay_back.wait()
-    for field in range(4):
-        all_over(field).wait_send()
-        gather_all(field).wait_send()
-    for field in range(3):
-        for piece in range(PIECES[field]):
-            all_across(field, piece).wait_send()
+    remote(relay, relay, relay_send, relay_recv.at[0], ky=partner).wait_send()
+    sent = gathered.at[:, :, pl.ds(0, (ky_count - 2) * rows)]
+    remote(sent, sent, gather_send, gather_recv.at[0], ky=partner).wait_send()
+    sent = across.at[:, :, :, pl.ds(0, N - part)]
+    remote(sent, sent, kz_send, kz_recv.at[0], kz=kz_peers()[0]).wait_send()
     over.wait_send()
     back.wait_send()
 
@@ -372,7 +376,6 @@
     rows, part = fields.shape[3], fields.shape[4]
     in_vmem = lambda *shape: pltpu.VMEM(shape, BF16)
     dma = lambda *shape: pltpu.SemaphoreType.DMA(shape)
-    most = max(PIECES)
     vmem, hbm = pl.BlockSpec(memory_space=pltpu.VMEM), pl.BlockSpec(memory_space=pltpu.HBM)
     shape = lambda *dims: jax.ShapeDtypeStruct(dims, BF16)
     scalar_shape = shape(2, ky_count, rows, part)
@@ -380,9 +383,10 @@
     held = pl.pallas_call(
         functools.partial(kernel, ky_count, kz_count),
         out_shape=(shape(3, 2, part, N), scalar_shape, shape(2, piece, N), shape(N, N), shape(N, N)),
-        in_specs=[pl.BlockSpec(memory_space=pltpu.SMEM), pl.BlockSpec(memory_space=pl.ANY)],
+        in_specs=[hbm, pl.BlockSpec(memory_space=pl.ANY)],
         out_specs=(vmem,) * 5,
         scratch_shapes=[
+            pltpu.SMEM((ky_count,), jnp.int32),
             in_vmem(4, 2, N, part),
             in_vmem(4, 2, ky_count // 2, rows, part),
             in_vmem(2, N, part),
@@ -394,15 +398,16 @@
             in_vmem(N, N),
             in_vmem(N, N),
             pltpu.SemaphoreType.REGULAR((ROUNDS,)),
+            pltpu.SemaphoreType.DMA,
+            pltpu.SemaphoreType.DMA,
             dma(4),
             dma(4),
+            pltpu.SemaphoreType.DMA,
             dma(4),
             dma(4),
-            dma(4),
-            dma(4),
-            dma(3, most),
-            dma(3, most),
-            dma(3, most),
+            pltpu.SemaphoreType.DMA,
+            dma(sum(PIECES)),
+            dma(sum(PIECES)),
             pltpu.SemaphoreType.DMA,
             pltpu.SemaphoreType.DMA,
             pltpu.SemaphoreType.DMA,

time: 102 us -> 101 us (level)
  no operation moved by 1% of the time
where the time goes in v3:
time: 101 us
  Pallas kernels  99.3 us (98%)
    pallas_call x1, Pallas kernels, shards(): pl.pallas_call(functools.partial(kernel, ky_count, kz_count), out_shape=(...  97.2 us
    pallas_call x1, Pallas kernels, shards(): pl.pallas_call(functools.partial(finish, kz_count), out_shape=(shape(3, 2...  2.09 us

profile of v3, /device:TPU:1, one launch (start us, length us, event | category | flops | bytes accessed | tf_op | source)
XLA Modules:
  0.0 100.6 jit_solution(3932211654934616118)
XLA Ops:
  0.6 0.0 copy-start
  0.6 0.6 copy-done
  1.3 97.2 %roll_and_transform.1 = (bf16[3,2,256,1024]{3,2,1,0:T(8,128)(2,1)S(1)}, bf16[2,32,32,256]{3,2,1,0:T(8,128)(2,1)S(1)}, bf16[2,64,1024]{2,1,0:T(8,128)(2,1)S(1)}, ...) custom-call(s32[32]{0:T(128)S(1)} %copy-done, bf16[4,2,32,32,256]{4,3,2,1,0:T(8,128)(2,1)} %fields_ref.1), custom_call_target="tpu_custom_call" | custom-call | tf_op jit(solution)/shard_map/roll_and_transform/pallas_call | solution.py:383
  98.5 2.1 %finish.1 = (bf16[3,2,1,256,1024]{4,3,2,1,0:T(8,128)(2,1)}, bf16[2,32,32,256]{3,2,1,0:T(8,128)(2,1)}) custom-call(bf16[3,2,256,1024]{3,2,1,0:T(8,128)(2,1)S(1)} %get-tuple-element.7.velocity_ref, bf16[2,32,32,256]{3,2,1,0:T(8,128)(2,1)S(1)} %get-tuple-element.8.scalar_ref, bf16[2,64,1024]{2,1,0:T(8,128)(2,1)S(1)} %get-tuple-element.9.last_ref, ...), custom_call_target="tpu_custom_call" | custom-call | tf_op jit(solution)/shard_map/finish/pallas_call | solution.py:422
Async XLA Ops:
  0.6 0.7 copy-start

commit v4 on v3

--- a/solution.py
+++ b/solution.py
@@ -374,6 +374,7 @@
 def shards(fields, offsets):
     ky_count, kz_count = lax.axis_size("ky"), lax.axis_size("kz")
     rows, part = fields.shape[3], fields.shape[4]
+    in_hbm = lambda array: pltpu.with_memory_space_constraint(array, pltpu.HBM)
     in_vmem = lambda *shape: pltpu.VMEM(shape, BF16)
     dma = lambda *shape: pltpu.SemaphoreType.DMA(shape)
     vmem, hbm = pl.BlockSpec(memory_space=pltpu.VMEM), pl.BlockSpec(memory_space=pltpu.HBM)
@@ -418,7 +419,7 @@
             collective_id=0, has_side_effects=True, vmem_limit_bytes=44 * 2**20
         ),
         name="roll_and_transform",
-    )(offsets, fields)
+    )(in_hbm(offsets), in_hbm(fields))
     return pl.pallas_call(
         functools.partial(finish, kz_count),
         out_shape=(shape(3, 2, 1, part, N), scalar_shape),

time: 101 us -> 100 us (0.990)
  no operation moved by 1% of the time
where the time goes in v4:
time: 100 us
  Pallas kernels  99.4 us (99%)
    pallas_call x1, Pallas kernels, shards(): pl.pallas_call(functools.partial(kernel, ky_count, kz_count), out_shape=(...  97.3 us
    pallas_call x1, Pallas kernels, shards(): pl.pallas_call(functools.partial(finish, kz_count), out_shape=(shape(3, 2...  2.1 us

profile of v4, /device:TPU:1, one launch (start us, length us, event | category | flops | bytes accessed | tf_op | source)
XLA Modules:
  0.0 100.1 jit_solution(9431252763229771937)
XLA Ops:
  0.6 97.3 %roll_and_transform.1 = (bf16[3,2,256,1024]{3,2,1,0:T(8,128)(2,1)S(1)}, bf16[2,32,32,256]{3,2,1,0:T(8,128)(2,1)S(1)}, bf16[2,64,1024]{2,1,0:T(8,128)(2,1)S(1)}, ...) custom-call(s32[32]{0:T(128)} %offsets_hbm.1, bf16[4,2,32,32,256]{4,3,2,1,0:T(8,128)(2,1)} %fields_ref.1), custom_call_target="tpu_custom_call" | custom-call | tf_op jit(solution)/shard_map/roll_and_transform/pallas_call | solution.py:384
  98.0 2.1 %finish.1 = (bf16[3,2,1,256,1024]{4,3,2,1,0:T(8,128)(2,1)}, bf16[2,32,32,256]{3,2,1,0:T(8,128)(2,1)}) custom-call(bf16[3,2,256,1024]{3,2,1,0:T(8,128)(2,1)S(1)} %get-tuple-element.7.velocity_ref, bf16[2,32,32,256]{3,2,1,0:T(8,128)(2,1)S(1)} %get-tuple-element.8.scalar_ref, bf16[2,64,1024]{2,1,0:T(8,128)(2,1)S(1)} %get-tuple-element.9.last_ref, ...), custom_call_target="tpu_custom_call" | custom-call | tf_op jit(solution)/shard_map/finish/pallas_call | solution.py:423

commit v5 on v4

--- a/solution.py
+++ b/solution.py
@@ -348,6 +348,18 @@
 
     for field in range(3):
         for piece in range(PIECES[field]):
+            if (field, piece) == LAST:
+                others_back = scalar_ref.at[:, pl.ds(0, ky_count - 2)]
+                back = remote(others_back, others_back, back_send, back_recv, ky=partner)
+                back.wait_recv()
+                own_back.wait()
+                relay_back.wait()
+                remote(relay, relay, relay_send, relay_recv.at[0], ky=partner).wait_send()
+                sent = gathered.at[:, :, pl.ds(0, (ky_count - 2) * rows)]
+                remote(sent, sent, gather_send, gather_recv.at[0], ky=partner).wait_send()
+                over.wait_send()
+                back.wait_send()
+
             own_across(field, piece).wait()
             all_across(field, piece).wait_recv()
             if (field, piece) != LAST:
@@ -357,18 +369,8 @@
                 )
 
     last_ref[...] = across[LAST[0], :, piece_rows(*LAST)]
-    others_back = scalar_ref.at[:, pl.ds(0, ky_count - 2)]
-    back = remote(others_back, others_back, back_send, back_recv, ky=partner)
-    back.wait_recv()
-    own_back.wait()
-    relay_back.wait()
-    remote(relay, relay, relay_send, relay_recv.at[0], ky=partner).wait_send()
-    sent = gathered.at[:, :, pl.ds(0, (ky_count - 2) * rows)]
-    remote(sent, sent, gather_send, gather_recv.at[0], ky=partner).wait_send()
     sent = across.at[:, :, :, pl.ds(0, N - part)]
     remote(sent, sent, kz_send, kz_recv.at[0], kz=kz_peers()[0]).wait_send()
-    over.wait_send()
-    back.wait_send()
 
 
 def shards(fields, offsets):

time: 100 us -> 100 us (level)
  no operation moved by 1% of the time
where the time goes in v5:
time: 100 us
  Pallas kernels  99.4 us (99%)
    pallas_call x1, Pallas kernels, shards(): pl.pallas_call(functools.partial(kernel, ky_count, kz_count), out_shape=(...  97.3 us
    pallas_call x1, Pallas kernels, shards(): pl.pallas_call(functools.partial(finish, kz_count), out_shape=(shape(3, 2...  2.09 us

profile of v5, /device:TPU:1, one launch (start us, length us, event | category | flops | bytes accessed | tf_op | source)
XLA Modules:
  0.0 100.1 jit_solution(8319536031394800327)
XLA Ops:
  0.6 97.3 %roll_and_transform.1 = (bf16[3,2,256,1024]{3,2,1,0:T(8,128)(2,1)S(1)}, bf16[2,32,32,256]{3,2,1,0:T(8,128)(2,1)S(1)}, bf16[2,64,1024]{2,1,0:T(8,128)(2,1)S(1)}, ...) custom-call(s32[32]{0:T(128)} %offsets_hbm.1, bf16[4,2,32,32,256]{4,3,2,1,0:T(8,128)(2,1)} %fields_ref.1), custom_call_target="tpu_custom_call" | custom-call | tf_op jit(solution)/shard_map/roll_and_transform/pallas_call | solution.py:386
  98.0 2.1 %finish.1 = (bf16[3,2,1,256,1024]{4,3,2,1,0:T(8,128)(2,1)}, bf16[2,32,32,256]{3,2,1,0:T(8,128)(2,1)}) custom-call(bf16[3,2,256,1024]{3,2,1,0:T(8,128)(2,1)S(1)} %get-tuple-element.7.velocity_ref, bf16[2,32,32,256]{3,2,1,0:T(8,128)(2,1)S(1)} %get-tuple-element.8.scalar_ref, bf16[2,64,1024]{2,1,0:T(8,128)(2,1)S(1)} %get-tuple-element.9.last_ref, ...), custom_call_target="tpu_custom_call" | custom-call | tf_op jit(solution)/shard_map/finish/pallas_call | solution.py:425

commit v6 on v5

--- a/solution.py
+++ b/solution.py
@@ -15,8 +15,8 @@
 BF16 = jnp.bfloat16
 F32 = jnp.float32
 SCALAR = 3
-PIECES = (1, 1, 4)
-FIRST = (0, 1, 2)
+PIECES = (2, 2, 4)
+FIRST = (0, 2, 4)
 LAST = (2, 3)
 ROUNDS = 7
 

time: 100 us -> 100 us (level)
  no operation moved by 1% of the time
where the time goes in v6:
time: 100 us
  Pallas kernels  99.5 us (100%)
    pallas_call x1, Pallas kernels, shards(): pl.pallas_call(functools.partial(kernel, ky_count, kz_count), out_shape=(...  97.4 us
    pallas_call x1, Pallas kernels, shards(): pl.pallas_call(functools.partial(finish, kz_count), out_shape=(shape(3, 2...  2.1 us

profile of v6, /device:TPU:1, one launch (start us, length us, event | category | flops | bytes accessed | tf_op | source)
XLA Modules:
  0.0 100.1 jit_solution(6863668548110167556)
XLA Ops:
  0.6 97.4 %roll_and_transform.1 = (bf16[3,2,256,1024]{3,2,1,0:T(8,128)(2,1)S(1)}, bf16[2,32,32,256]{3,2,1,0:T(8,128)(2,1)S(1)}, bf16[2,64,1024]{2,1,0:T(8,128)(2,1)S(1)}, ...) custom-call(s32[32]{0:T(128)} %offsets_hbm.1, bf16[4,2,32,32,256]{4,3,2,1,0:T(8,128)(2,1)} %fields_ref.1), custom_call_target="tpu_custom_call" | custom-call | tf_op jit(solution)/shard_map/roll_and_transform/pallas_call | solution.py:386
  98.0 2.1 %finish.1 = (bf16[3,2,1,256,1024]{4,3,2,1,0:T(8,128)(2,1)}, bf16[2,32,32,256]{3,2,1,0:T(8,128)(2,1)}) custom-call(bf16[3,2,256,1024]{3,2,1,0:T(8,128)(2,1)S(1)} %get-tuple-element.7.velocity_ref, bf16[2,32,32,256]{3,2,1,0:T(8,128)(2,1)S(1)} %get-tuple-element.8.scalar_ref, bf16[2,64,1024]{2,1,0:T(8,128)(2,1)S(1)} %get-tuple-element.9.last_ref, ...), custom_call_target="tpu_custom_call" | custom-call | tf_op jit(solution)/shard_map/finish/pallas_call | solution.py:425
